TPU v7x, 32 devices: a whole 2x2x4 slice. The times are simulated.
32 devices in a mesh: groups: 2 (over y), tensor: 16 (over z, x, core).
Axes of the slice: x: 2, y: 2, z: 4, core: 2. Of those that a mesh axis runs over, the one named last changes fastest.
Arguments:
- inputs: bfloat16 [256, 8192], P('groups', 'tensor'), parts along dimension 0, may hold values from -6 to 6
- gate_weight: bfloat16 [8192, 28672], P(None, 'tensor'), may hold values from -0.09375 to 0.09375
- up_weight: bfloat16 [8192, 28672], P(None, 'tensor'), may hold values from -0.09375 to 0.09375
- down_weight: bfloat16 [28672, 8192], P('tensor'), may hold values from -0.03125 to 0.03125
- cotangent: bfloat16 [4, 256, 8192], P(None, 'groups', 'tensor'), parts along dimension 1, may hold values from -6 to 6
- threshold_levels: int32 [28672], P('tensor'), may hold values from 4 to 16
- membrane_offsets: int32 [256, 28672], P('groups', 'tensor'), parts along dimension 0, may hold values from 0 to 255
Outputs:
- grad_input: float32 [256, 8192], P('groups', 'tensor'), parts along dimension 0
- grad_threshold: float32 [57344], P(('groups', 'tensor')), parts along dimension 0
There are 2 independent parts, one for each index of `groups`. A program takes and returns all parts, laid end to end along the dimension named above; an argument that names none is the same for every part. Nothing has to cross between parts.
All inputs are finite; a program needn't handle non-finite values.
Results may differ from a plain program's by a relative error of at most 0.0031.
Values may be sent and summed in bfloat16 or wider, within the bound.
No kernel may reach another device: no remote copies, remote signals or barrier semaphores. Data moves between devices by JAX's collectives and lax.ppermute only.
A program may use at most 256 MiB of HBM per device.

v0:
```python
import jax
import jax.numpy as jnp
from jax import lax
from jax.sharding import PartitionSpec as P

slope_gain = 4.0


def transposed_product(left, weight):
    return lax.dot_general(
        left, weight, (((1,), (1,)), ((), ())), preferred_element_type=jnp.float32
    )


def body(
    inputs, gate_weight, up_weight, down_weight, cotangent, threshold_levels, membrane_offsets
):
    step_count = cotangent.shape[0]
    piece = lax.all_gather(inputs, "tensor", axis=1, tiled=True)
    gate = jnp.dot(piece, gate_weight, preferred_element_type=jnp.float32)
    up = jnp.dot(piece, up_weight, preferred_element_type=jnp.float32)
    feedback_all = jnp.einsum(
        "tkd,fd->tkf",
        lax.all_gather(cotangent, "tensor", axis=2, tiled=True),
        down_weight,
        preferred_element_type=jnp.float32,
    )
    theta = threshold_levels.astype(jnp.float32) / 8.0
    sig = jax.nn.sigmoid(gate)
    current = gate * sig * up
    dsilu = sig * (1.0 + gate * (1.0 - sig))
    offset_share = membrane_offsets.astype(jnp.float32) / 256.0
    membrane = theta * offset_share
    spikes = []
    for step in range(step_count):
        pre = membrane + current
        spike = jax.nn.sigmoid(slope_gain * (pre - theta))
        spikes.append(spike)
        membrane = pre - theta * spike
    later = jnp.zeros_like(current)
    grad_threshold = jnp.zeros(theta.shape, jnp.float32)
    collected = []
    for step in range(step_count - 1, -1, -1):
        feedback = feedback_all[step]
        spike = spikes[step]
        dspike = theta * (feedback - later)
        slope = slope_gain * spike * (1.0 - spike)
        dpre = dspike * slope + later
        grad_threshold = grad_threshold + jnp.sum(
            feedback * spike - later * spike - dspike * slope, axis=0
        )
        dgate = (dpre * up * dsilu).astype(jnp.bfloat16)
        dup = (dpre * gate * sig).astype(jnp.bfloat16)
        term = transposed_product(dgate, gate_weight) + transposed_product(dup, up_weight)
        collected.append(lax.psum_scatter(term, "tensor", scatter_dimension=1, tiled=True))
        later = dpre
    grad_threshold = grad_threshold + jnp.sum(later * offset_share, axis=0)
    grad_input = collected[0]
    for part_sum in collected[1:]:
        grad_input = grad_input + part_sum
    return (grad_input, grad_threshold)


def solution(mesh):
    placed = (
        P("groups", "tensor"),
        P(None, "tensor"),
        P(None, "tensor"),
        P("tensor", None),
        P(None, "groups", "tensor"),
        P("tensor"),
        P("groups", "tensor"),
    )
    return jax.shard_map(
        body,
        mesh=mesh,
        in_specs=placed,
        out_specs=(P("groups", "tensor"), P(("groups", "tensor"))),
        check_vma=False,
    )
```

profile of v0, /device:TPU:0, one launch (start us, length us, event | category | flops | bytes accessed | tf_op | source)
XLA Modules:
  0.0 368.1 jit_solution(3617723521399008605)
XLA Ops:
  7.2 0.0 all-gather.5.cloned.1.call-start
  7.2 0.7 all-gather.5.cloned.1.call-update
  7.9 0.0 all-gather.3.cloned.1.call-start
  7.9 0.7 all-gather.3.cloned.1.call-update
  8.6 0.0 reduce-scatter.2.cloned.1.call-start
  8.7 0.7 convert_multiply_fusion
  9.4 0.0 copy-start.3
  9.4 44.7 %all-gather.5.cloned.1.call-done = bf16[128,8192]{1,0:T(8,128)(2,1)} async-done(((bf16[128,512]{1,0:T(8,128)(2,1)}), bf16[128,8192]{1,0:T(8,128)(2,1)}) %all-gather.5.cloned.1.call-update) | async-done | bytes 2097168 | tf_op jit(solution)/shard_map/all_gather | solution.py:19
  54.1 0.0 copy-start.2
  54.1 14.8 %fusion.19 = f32[128,1792]{1,0:T(8,128)S(1)} fusion(bf16[128,8192]{1,0:T(8,128)(2,1)} %all-gather.5.cloned.1.call-done, bf16[8192,1792]{1,0:T(8,128)(2,1)} %param.8), kind=kOutput, calls=%fused_computation.54 | convolution fusion | flops 3758096384 | bytes 32374784 | tf_op jit(solution)/shard_map/dot_general | solution.py:20
  68.9 0.0 copy-done.3
  68.9 0.0 copy-done.2
  68.9 15.9 %add_divide_fusion = (f32[128,1792]{1,0:T(8,128)}, f32[128,1792]{1,0:T(8,128)}, f32[128,1792]{1,0:T(8,128)S(1)}) fusion(f32[1792]{0:T(1024)S(1)} %get-tuple-element.14, f32[1792]{0:T(1024)S(1)} %get-tuple-element.13, s32[128,1792]{1,0:T(8,128)S(1)} %copy-done.3, f32[128,1792]{1,0:T(8,128)S(1)} %fusion.19, bf16[128,8192]{1,0:T(8,128)(2,1)S(1)} %copy-done.2, ...), kind=kOutput, calls=%fused_computation.34 | convolution fusion | flops 3766583296 | bytes 36059136 | tf_op jit(solution)/shard_map/dot_general | solution.py:21
  84.8 48.5 %all-gather.3.cloned.1.call-done = bf16[4,128,8192]{2,1,0:T(8,128)(2,1)} async-done(((bf16[4,128,512]{2,1,0:T(8,128)(2,1)}), bf16[4,128,8192]{2,1,0:T(8,128)(2,1)}) %all-gather.3.cloned.1.call-update) | async-done | bytes 8388624 | tf_op jit(solution)/shard_map/all_gather | solution.py:24
  133.3 23.0 %fusion = f32[4,128,1792]{2,1,0:T(8,128)} fusion(bf16[4,128,8192]{2,1,0:T(8,128)(2,1)} %all-gather.3.cloned.1.call-done, bf16[1792,8192]{1,0:T(8,128)(2,1)} %param.10), kind=kOutput, calls=%fused_computation | convolution fusion | flops 15032385536 | bytes 41418752 | tf_op jit(solution)/shard_map/tkd,fd->tkf/dot_general | solution.py:22
  156.3 0.0 copy-done.4
  156.3 0.0 copy-done.5
  156.3 0.0 copy-done.6
  156.3 4.8 %subtract_reduce_fusion.2 = (f32[1792]{0:T(1024)S(1)}, f32[1792]{0:T(1024)S(1)}, f32[1792]{0:T(1024)S(1)}, f32[1792]{0:T(1024)S(1)}, f32[1792]{0:T(1024)S(1)}, /...) fusion(f32[4,128,1792]{2,1,0:T(8,128)} %fusion, ...), kind=kLoop, calls=%fused_computation.16 | loop fusion | flops 16735488 | bytes 10142720 | tf_op jit(solution)/shard_map/reduce_sum | solution.py:49
  161.0 1.0 copy-done
  162.0 14.3 %fusion.11 = f32[128,8192]{1,0:T(8,128)S(1)} fusion(bf16[8192,1792]{1,0:T(8,128)(2,1)} %param.8, f32[128,1792]{1,0:T(8,128)S(1)} %get-tuple-element.7, f32[128,1792]{1,0:T(8,128)S(1)} %get-tuple-element.15, f32[128,1792]{1,0:T(8,128)S(1)} %fusion.19), kind=kOutput, calls=%fused_computation.46 | convolution fusion | flops 3760390144 | bytes 36306944 | tf_op jit(solution)/shard_map/dot_general | solution.py:10
  176.3 15.9 %convolution_add_fusion = f32[128,8192]{1,0:T(8,128)} fusion(f32[128,8192]{1,0:T(8,128)S(1)} %fusion.11, bf16[8192,1792]{1,0:T(8,128)(2,1)} %param.9, f32[128,1792]{1,0:T(8,128)} %copy-done, f32[128,1792]{1,0:T(8,128)S(1)} %fusion.19), kind=kOutput, calls=%fused_computation.2 | convolution fusion | flops 3760521216 | bytes 39583744 | tf_op jit(solution)/shard_map/dot_general | solution.py:10
  192.2 14.4 %fusion.10 = f32[128,8192]{1,0:T(8,128)S(1)} fusion(bf16[8192,1792]{1,0:T(8,128)(2,1)} %param.8, f32[128,1792]{1,0:T(8,128)} %get-tuple-element.8, f32[128,1792]{1,0:T(8,128)S(1)} %get-tuple-element.15, f32[128,1792]{1,0:T(8,128)S(1)} %fusion.19), kind=kOutput, calls=%fused_computation.45 | convolution fusion | flops 3760390144 | bytes 36306944 | tf_op jit(solution)/shard_map/dot_general | solution.py:10
  206.7 16.0 %convolution_add_fusion.1 = f32[128,8192]{1,0:T(8,128)} fusion(f32[128,8192]{1,0:T(8,128)S(1)} %fusion.10, bf16[8192,1792]{1,0:T(8,128)(2,1)} %param.9, f32[128,1792]{1,0:T(8,128)} %get-tuple-element.8, f32[128,1792]{1,0:T(8,128)S(1)} %fusion.19), kind=kOutput, calls=%fused_computation.3 | convolution fusion | flops 3760521216 | bytes 39583744 | tf_op jit(solution)/shard_map/dot_general | solution.py:10
  222.6 14.2 %fusion.9 = f32[128,8192]{1,0:T(8,128)S(1)} fusion(bf16[8192,1792]{1,0:T(8,128)(2,1)} %param.8, f32[128,1792]{1,0:T(8,128)S(1)} %get-tuple-element.9, f32[128,1792]{1,0:T(8,128)S(1)} %get-tuple-element.15, f32[128,1792]{1,0:T(8,128)S(1)} %fusion.19), kind=kOutput, calls=%fused_computation.44 | convolution fusion | flops 3760390144 | bytes 36306944 | tf_op jit(solution)/shard_map/dot_general | solution.py:10
  236.9 16.7 %convolution_add_fusion.2 = f32[128,8192]{1,0:T(8,128)} fusion(f32[128,8192]{1,0:T(8,128)S(1)} %fusion.9, bf16[8192,1792]{1,0:T(8,128)(2,1)} %param.9, f32[128,1792]{1,0:T(8,128)S(1)} %get-tuple-element.9, f32[128,1792]{1,0:T(8,128)S(1)} %fusion.19), kind=kOutput, calls=%fused_computation.4 | convolution fusion | flops 3760521216 | bytes 39583744 | tf_op jit(solution)/shard_map/dot_general | solution.py:10
  253.6 18.2 %fusion.8 = f32[128,8192]{1,0:T(8,128)} fusion(bf16[8192,1792]{1,0:T(8,128)(2,1)} %param.8, f32[128,1792]{1,0:T(8,128)} %get-tuple-element.10, f32[128,1792]{1,0:T(8,128)S(1)} %get-tuple-element.15, f32[128,1792]{1,0:T(8,128)S(1)} %fusion.19), kind=kOutput, calls=%fused_computation.43 | convolution fusion | flops 3760390144 | bytes 36306944 | tf_op jit(solution)/shard_map/dot_general | solution.py:10
  271.7 0.0 copy-done.1
  271.7 19.2 %fusion.4 = f32[128,8192]{1,0:T(8,128)} fusion(f32[128,8192]{1,0:T(8,128)} %convolution_add_fusion, f32[128,8192]{1,0:T(8,128)} %convolution_add_fusion.1, f32[128,8192]{1,0:T(8,128)} %convolution_add_fusion.2, f32[128,8192]{1,0:T(8,128)} %fusion.8, bf16[8192,1792]{1,0:T(8,128)(2,1)} %param.9, f32[128,1792]{1,0:T(8,128)S(1)} %copy-done.1, ...), kind=kOutput, calls=%fused_computation.8 | convolution fusion | flops 3763666944 | bytes 52166656 | tf_op jit(solution)/shard_map/dot_general | solution.py:10
  290.9 0.0 reduce-scatter.2.cloned.1.call-update
  291.0 0.6 add_add_fusion
  291.6 70.0 %reduce-scatter.2.cloned.1.call-done = f32[128,512]{1,0:T(8,128)} async-done(((f32[128,8192]{1,0:T(8,128)}), f32[128,512]{1,0:T(8,128)}) %reduce-scatter.2.cloned.1.call-update) | async-done | bytes 262160 | tf_op jit(solution)/shard_map/reduce_scatter | solution.py:55
  (5 shorter events, 0.0 us)
Async XLA Ops:
  7.2 46.9 %all-gather.5.cloned.1.call-start = ((), (), s32[]{:S(2)}) async-start(), calls=%async_computation.2 | async-start | bytes 2228224 | tf_op jit(solution)/shard_map/all_gather | solution.py:19
  7.9 125.4 %all-gather.3.cloned.1.call-start = ((), (), s32[]{:S(2)}) async-start(), calls=%async_computation.1 | async-start | bytes 8912896 | tf_op jit(solution)/shard_map/all_gather | solution.py:24
  8.6 353.0 %reduce-scatter.2.cloned.1.call-start = ((), (), s32[]{:S(2)}) async-start(), calls=%async_computation.3 | async-start | bytes 4456448 | tf_op jit(solution)/shard_map/reduce_scatter | solution.py:55
  9.4 59.5 %copy-start.3 = (s32[128,1792]{1,0:T(8,128)S(1)}, s32[128,1792]{1,0:T(8,128)}, u32[]{:S(2)}) copy-start(s32[128,1792]{1,0:T(8,128)} %param.13) | copy-start | bytes 2752516
  54.1 14.8 %copy-start.2 = (bf16[128,8192]{1,0:T(8,128)(2,1)S(1)}, bf16[128,8192]{1,0:T(8,128)(2,1)}, u32[]{:S(2)}) copy-start(bf16[128,8192]{1,0:T(8,128)(2,1)} %all-gather.5.cloned.1.call-done) | copy-start | bytes 6291460
  133.3 23.0 %copy-start.4 = (s32[128,1792]{1,0:T(8,128)S(1)}, s32[128,1792]{1,0:T(8,128)}, u32[]{:S(2)}) copy-start(s32[128,1792]{1,0:T(8,128)} %param.13) | copy-start | bytes 2752516
  133.3 23.0 %copy-start.5 = (f32[128,1792]{1,0:T(8,128)S(1)}, f32[128,1792]{1,0:T(8,128)}, u32[]{:S(2)}) copy-start(f32[128,1792]{1,0:T(8,128)} %get-tuple-element.11) | copy-start | bytes 2752516
  133.3 23.0 %copy-start.6 = (f32[128,1792]{1,0:T(8,128)S(1)}, f32[128,1792]{1,0:T(8,128)}, u32[]{:S(2)}) copy-start(f32[128,1792]{1,0:T(8,128)} %get-tuple-element.12) | copy-start | bytes 2752516
  161.0 1.0 copy-start
  253.6 18.2 %copy-start.1 = (f32[128,1792]{1,0:T(8,128)S(1)}, f32[128,1792]{1,0:T(8,128)}, u32[]{:S(2)}) copy-start(f32[128,1792]{1,0:T(8,128)} %get-tuple-element.10) | copy-start | bytes 2752516
Sparse Core Ops, SparseCore 0:
  10.2 43.8 all-gather.4
  56.2 77.0 all-gather.2
  291.1 70.4 reduce-scatter.1
where the time goes:
time: 369 us; the launch traced here: 368 us
  matrix products  183 us (50%)
  waiting for transfers between devices  165 us (45%)
  between operations  13.8 us (4%)
  other arithmetic  6.08 us (2%)
    dot_general x8, matrix products, transposed_product(): lax.dot_general(left, weight, (((1,), (1,)), ((), ())), preferred_element...  129 us
    reduce_scatter x1, waiting for transfers between devices, body(): lax.psum_scatter(term, 'tensor', scatter_dimension=1, tiled=True)  70 us
    all_gather x1, waiting for transfers between devices, body(): lax.all_gather(cotangent, 'tensor', axis=2, tiled=True)  48.5 us
    all_gather x1, waiting for transfers between devices, body(): piece = lax.all_gather(inputs, 'tensor', axis=1, tiled=True)  44.7 us
    dot_general x1, matrix products, body(): jnp.einsum('tkd,fd->tkf', lax.all_gather(cotangent, 'tensor', axis=2, til...  23 us
    dot_general x1, matrix products, body(): up = jnp.dot(piece, up_weight, preferred_element_type=jnp.float32)  15.9 us
    dot_general x1, matrix products, body(): gate = jnp.dot(piece, gate_weight, preferred_element_type=jnp.float32)  14.8 us
  transfers between devices with their start and end apart: 3, of which 3 were waited for; matrix products, arithmetic and copies ran while one was open for 9% of the time, Pallas kernels for 0%

commit v1 on v0

--- a/solution.py
+++ b/solution.py
@@ -4,6 +4,19 @@
 from jax.sharding import PartitionSpec as P
 
 slope_gain = 4.0
+
+
+def gather_around(shard, axis, dim):
+    ways = lax.axis_size(axis)
+    up = [(d, (d + 1) % ways) for d in range(ways)]
+    down = [(d, (d - 1) % ways) for d in range(ways)]
+    earlier, later = ([shard], [shard])
+    for _ in range(ways // 2):
+        earlier.append(lax.ppermute(earlier[-1], axis, up))
+    for _ in range((ways - 1) // 2):
+        later.append(lax.ppermute(later[-1], axis, down))
+    line = jnp.concatenate([*earlier[::-1], *later[1:]], axis=dim)
+    return jnp.roll(line, (lax.axis_index(axis) - ways // 2) * shard.shape[dim], axis=dim)
 
 
 def transposed_product(left, weight):
@@ -21,7 +34,7 @@
     up = jnp.dot(piece, up_weight, preferred_element_type=jnp.float32)
     feedback_all = jnp.einsum(
         "tkd,fd->tkf",
-        lax.all_gather(cotangent, "tensor", axis=2, tiled=True),
+        gather_around(cotangent, "tensor", 2),
         down_weight,
         preferred_element_type=jnp.float32,
     )

time: 369 us -> 415 us (1.12)
  starting transfers between devices: 0.11 us -> 69.3 us
  waiting for transfers between devices: 165 us -> 109 us
  local copies, waits for them, and re-layouts: 1.01 us -> 37.4 us
  matrix products: 183 us -> 178 us
    ppermute x0 -> x15, starting transfers between devices: none -> 69.2 us  [the longest x8 60.3 us: gather_around(): earlier.append(lax.ppermute(earlier[-1], axis, up))]
    all_gather x1 -> x0, waiting for transfers between devices: 48.5 us -> none  [body(): lax.all_gather(cotangent, 'tensor', axis=2, tiled=True)]
    all_gather x1, waiting for transfers between devices: 44.7 us -> 0.01 us  [body(): piece = lax.all_gather(inputs, 'tensor', axis=1, tiled=True)]
    unnamed x14 -> x73, local copies, waits for them, and re-layouts: 1.01 us -> 35.5 us
    ppermute x0 -> x15, waiting for transfers between devices: none -> 33.4 us  [the longest x8 33.4 us: gather_around(): earlier.append(lax.ppermute(earlier[-1], axis, up))]
    reduce_scatter x1, waiting for transfers between devices: 70 us -> 74.9 us  [body(): lax.psum_scatter(term, 'tensor', scatter_dimension=1, tiled=True)]
  transfers between devices with their start and end apart: 3 -> 17, of which waited for: 3 -> 8; matrix products, arithmetic and copies ran while one was open for 9% -> 11% of each run, Pallas kernels for 0% -> 0%
where the time goes in v1:
time: 415 us
  matrix products  178 us (43%)
  waiting for transfers between devices  109 us (26%)
  starting transfers between devices  69.3 us (17%)
  local copies, waits for them, and re-layouts  37.4 us (9%)
  between operations  14.2 us (3%)
  other arithmetic  6.67 us (2%)
    dot_general x8, matrix products, transposed_product(): lax.dot_general(left, weight, (((1,), (1,)), ((), ())), preferred_element...  127 us
    reduce_scatter x1, waiting for transfers between devices, body(): lax.psum_scatter(term, 'tensor', scatter_dimension=1, tiled=True)  74.9 us
    ppermute x8, starting transfers between devices, gather_around(): earlier.append(lax.ppermute(earlier[-1], axis, up))  60.3 us
    unnamed x73, local copies, waits for them, and re-layouts  35.5 us
    ppermute x8, waiting for transfers between devices, gather_around(): earlier.append(lax.ppermute(earlier[-1], axis, up))  33.4 us
    dot_general x1, matrix products, body(): jnp.einsum('tkd,fd->tkf', gather_around(cotangent, 'tensor', 2), down_wei...  22.8 us
    dot_general x1, matrix products, body(): up = jnp.dot(piece, up_weight, preferred_element_type=jnp.float32)  15.8 us
    dot_general x1, matrix products, body(): gate = jnp.dot(piece, gate_weight, preferred_element_type=jnp.float32)  12.5 us
  transfers between devices with their start and end apart: 17, of which 8 were waited for; matrix products, arithmetic and copies ran while one was open for 11% of the time, Pallas kernels for 0%

profile of v1, /device:TPU:0, one launch (start us, length us, event | category | flops | bytes accessed | tf_op | source)
XLA Modules:
  0.0 414.6 jit_solution(3703976675616071929)
XLA Ops:
  8.4 5.0 %collective-permute-start.8 = (bf16[4,128,512]{2,1,0:T(8,128)(2,1)}, bf16[4,128,512]{2,1,0:T(8,128)(2,1)S(1)}, u32[]{:S(2)}, u32[]{:S(2)}) collective-permute-start(bf16[4,128,512]{2,1,0:T(8,128)(2,1)} %param.11), channel_id=1, source_target_pairs={{0,15},{1,0},{2,1},{3,2},{4,3},{5,4},{6,5},{7,6},{8,7},{9,8},{10,9... | collective-permute-start | bytes 1572872 | tf_op jit(solution)/shard_map/ppermute | solution.py:17
  13.5 7.1 %collective-permute-done = bf16[4,128,512]{2,1,0:T(8,128)(2,1)S(1)} collective-permute-done((bf16[4,128,512]{2,1,0:T(8,128)(2,1)}, bf16[4,128,512]{2,1,0:T(8,128)(2,1)S(1)}, u32[]{:S(2)}, u32[]{:S(2)}) %collective-permute-start) | collective-permute-done | bytes 524320 | tf_op jit(solution)/shard_map/ppermute | solution.py:15
  20.6 3.9 collective-permute-start.1
  25.1 11.0 %collective-permute-done.1 = bf16[4,128,512]{2,1,0:T(8,128)(2,1)S(1)} collective-permute-done((bf16[4,128,512]{2,1,0:T(8,128)(2,1)S(1)}, bf16[4,128,512]{2,1,0:T(8,128)(2,1)S(1)}, u32[]{:S(2)}, u32[]{:S(2)}) %collective-permute-start.1) | collective-permute-done | bytes 524320 | tf_op jit(solution)/shard_map/ppermute | solution.py:15
  38.0 2.6 collective-permute-start.10
  40.6 7.0 %collective-permute-done.2 = bf16[4,128,512]{2,1,0:T(8,128)(2,1)S(1)} collective-permute-done((bf16[4,128,512]{2,1,0:T(8,128)(2,1)S(1)}, bf16[4,128,512]{2,1,0:T(8,128)(2,1)S(1)}, u32[]{:S(2)}, u32[]{:S(2)}) %collective-permute-start.2) | collective-permute-done | bytes 524320 | tf_op jit(solution)/shard_map/ppermute | solution.py:15
  47.6 9.5 %collective-permute-start.3 = (bf16[4,128,512]{2,1,0:T(8,128)(2,1)S(1)}, bf16[4,128,512]{2,1,0:T(8,128)(2,1)S(1)}, u32[]{:S(2)}, u32[]{:S(2)}) collective-permute-start(bf16[4,128,512]{2,1,0:T(8,128)(2,1)S(1)} %collective-permute-done.2), channel_id=1, source_target_pairs={{0,1},{1,2},{2,3},{3,4},{4,5},{5,6},{6,7},{7,8},{8,9},{9,10},{10,1... | collective-permute-start | bytes 1572872 | tf_op jit(solution)/shard_map/ppermute | solution.py:15
  57.9 4.0 collective-permute-done.3
  61.9 8.9 %collective-permute-start.4 = (bf16[4,128,512]{2,1,0:T(8,128)(2,1)S(1)}, bf16[4,128,512]{2,1,0:T(8,128)(2,1)S(1)}, u32[]{:S(2)}, u32[]{:S(2)}) collective-permute-start(bf16[4,128,512]{2,1,0:T(8,128)(2,1)S(1)} %collective-permute-done.3), channel_id=1, source_target_pairs={{0,1},{1,2},{2,3},{3,4},{4,5},{5,6},{6,7},{7,8},{8,9},{9,10},{10,1... | collective-permute-start | bytes 1572872 | tf_op jit(solution)/shard_map/ppermute | solution.py:15
  73.4 10.6 %collective-permute-start.5 = (bf16[4,128,512]{2,1,0:T(8,128)(2,1)S(1)}, bf16[4,128,512]{2,1,0:T(8,128)(2,1)S(1)}, u32[]{:S(2)}, u32[]{:S(2)}) collective-permute-start(bf16[4,128,512]{2,1,0:T(8,128)(2,1)S(1)} %collective-permute-done.4), channel_id=1, source_target_pairs={{0,1},{1,2},{2,3},{3,4},{4,5},{5,6},{6,7},{7,8},{8,9},{9,10},{10,1... | collective-permute-start | bytes 1572872 | tf_op jit(solution)/shard_map/ppermute | solution.py:15
  85.6 12.7 %collective-permute-start.6 = (bf16[4,128,512]{2,1,0:T(8,128)(2,1)S(1)}, bf16[4,128,512]{2,1,0:T(8,128)(2,1)}, u32[]{:S(2)}, u32[]{:S(2)}) collective-permute-start(bf16[4,128,512]{2,1,0:T(8,128)(2,1)S(1)} %collective-permute-done.5), channel_id=1, source_target_pairs={{0,1},{1,2},{2,3},{3,4},{4,5},{5,6},{6,7},{7,8},{8,9},{9,10},{10,1... | collective-permute-start | bytes 1572872 | tf_op jit(solution)/shard_map/ppermute | solution.py:15
  99.9 12.4 %collective-permute-start.7 = (bf16[4,128,512]{2,1,0:T(8,128)(2,1)}, bf16[4,128,512]{2,1,0:T(8,128)(2,1)}, u32[]{:S(2)}, u32[]{:S(2)}) collective-permute-start(bf16[4,128,512]{2,1,0:T(8,128)(2,1)} %collective-permute-done.6), channel_id=1, source_target_pairs={{0,1},{1,2},{2,3},{3,4},{4,5},{5,6},{6,7},{7,8},{8,9},{9,10},{10,1... | collective-permute-start | bytes 1572872 | tf_op jit(solution)/shard_map/ppermute | solution.py:15
  112.3 12.5 %fusion.21 = f32[128,1792]{1,0:T(8,128)S(1)} fusion(bf16[128,8192]{1,0:T(8,128)(2,1)} %all-gather.2.cloned.1.call-done, bf16[8192,1792]{1,0:T(8,128)(2,1)} %param.8), kind=kOutput, calls=%fused_computation.88 | convolution fusion | flops 3758096384 | bytes 32374784 | tf_op jit(solution)/shard_map/dot_general | solution.py:33
  124.9 15.8 %add_divide_fusion = (f32[128,1792]{1,0:T(8,128)}, f32[128,1792]{1,0:T(8,128)}, f32[128,1792]{1,0:T(8,128)S(1)}) fusion(f32[1792]{0:T(1024)S(1)} %get-tuple-element.14, f32[1792]{0:T(1024)S(1)} %get-tuple-element.13, s32[128,1792]{1,0:T(8,128)S(1)} %copy-done.20, f32[128,1792]{1,0:T(8,128)S(1)} %fusion.21, bf16[128,8192]{1,0:T(8,128)(2,1)S(1)} %copy-done.2, ...), kind=kOutput, calls=%fused_computation.35 | convolution fusion | flops 3766583296 | bytes 36059136 | tf_op jit(solution)/shard_map/dot_general | solution.py:34
  142.6 1.9 constant_dynamic-update-slice_fusion.30
  154.6 1.9 constant_dynamic-update-slice_fusion.17
  156.5 1.9 constant_dynamic-update-slice_fusion.16
  158.4 1.9 constant_dynamic-update-slice_fusion.15
  160.3 1.9 constant_dynamic-update-slice_fusion.14
  172.4 1.9 constant_dynamic-update-slice_fusion.1
  174.3 1.9 constant_dynamic-update-slice_fusion
  176.2 22.8 %fusion = f32[4,128,1792]{2,1,0:T(8,128)} fusion(bf16[1792,8192]{1,0:T(8,128)(2,1)} %param.10, bf16[4,128,16384]{2,1,0:T(8,128)(2,1)} %constant_dynamic-update-slice_fusion, s32[]{:T(128)S(6)} %select_n.14), kind=kOutput, calls=%fused_computation | convolution fusion | flops 15032385536 | bytes 41418756 | tf_op jit(solution)/shard_map/tkd,fd->tkf/dot_general | solution.py:35
  199.0 5.4 %subtract_reduce_fusion.2 = (f32[1792]{0:T(1024)S(1)}, f32[1792]{0:T(1024)S(1)}, f32[1792]{0:T(1024)S(1)}, f32[1792]{0:T(1024)S(1)}, f32[1792]{0:T(1024)S(1)}, /...) fusion(f32[4,128,1792]{2,1,0:T(8,128)} %fusion, ...), kind=kLoop, calls=%fused_computation.17 | loop fusion | flops 16735488 | bytes 10142720 | tf_op jit(solution)/shard_map/reduce_sum | solution.py:62
  205.3 14.3 %fusion.10 = f32[128,8192]{1,0:T(8,128)S(1)} fusion(bf16[8192,1792]{1,0:T(8,128)(2,1)} %param.8, f32[128,1792]{1,0:T(8,128)S(1)} %get-tuple-element.9, f32[128,1792]{1,0:T(8,128)S(1)} %get-tuple-element.15, f32[128,1792]{1,0:T(8,128)S(1)} %fusion.21), kind=kOutput, calls=%fused_computation.45 | convolution fusion | flops 3760390144 | bytes 36306944 | tf_op jit(solution)/shard_map/dot_general | solution.py:23
  219.6 15.9 %convolution_add_fusion.2 = f32[128,8192]{1,0:T(8,128)} fusion(f32[128,8192]{1,0:T(8,128)S(1)} %fusion.10, bf16[8192,1792]{1,0:T(8,128)(2,1)} %param.9, f32[128,1792]{1,0:T(8,128)} %copy-done, f32[128,1792]{1,0:T(8,128)S(1)} %fusion.21), kind=kOutput, calls=%fused_computation.4 | convolution fusion | flops 3760521216 | bytes 39583744 | tf_op jit(solution)/shard_map/dot_general | solution.py:23
  235.5 14.5 %fusion.11 = f32[128,8192]{1,0:T(8,128)S(1)} fusion(bf16[8192,1792]{1,0:T(8,128)(2,1)} %param.8, f32[128,1792]{1,0:T(8,128)} %get-tuple-element.8, f32[128,1792]{1,0:T(8,128)S(1)} %get-tuple-element.15, f32[128,1792]{1,0:T(8,128)S(1)} %fusion.21), kind=kOutput, calls=%fused_computation.46 | convolution fusion | flops 3760390144 | bytes 36306944 | tf_op jit(solution)/shard_map/dot_general | solution.py:23
  250.0 15.9 %convolution_add_fusion.1 = f32[128,8192]{1,0:T(8,128)} fusion(f32[128,8192]{1,0:T(8,128)S(1)} %fusion.11, bf16[8192,1792]{1,0:T(8,128)(2,1)} %param.9, f32[128,1792]{1,0:T(8,128)} %get-tuple-element.8, f32[128,1792]{1,0:T(8,128)S(1)} %fusion.21), kind=kOutput, calls=%fused_computation.3 | convolution fusion | flops 3760521216 | bytes 39583744 | tf_op jit(solution)/shard_map/dot_general | solution.py:23
  265.9 15.5 %fusion.9 = f32[128,8192]{1,0:T(8,128)} fusion(bf16[8192,1792]{1,0:T(8,128)(2,1)} %param.8, f32[128,1792]{1,0:T(8,128)} %get-tuple-element.10, f32[128,1792]{1,0:T(8,128)S(1)} %get-tuple-element.15, f32[128,1792]{1,0:T(8,128)S(1)} %fusion.21), kind=kOutput, calls=%fused_computation.44 | convolution fusion | flops 3760390144 | bytes 36306944 | tf_op jit(solution)/shard_map/dot_general | solution.py:23
  281.5 14.2 %fusion.12 = f32[128,8192]{1,0:T(8,128)S(1)} fusion(bf16[8192,1792]{1,0:T(8,128)(2,1)} %param.8, f32[128,1792]{1,0:T(8,128)S(1)} %get-tuple-element.7, f32[128,1792]{1,0:T(8,128)S(1)} %get-tuple-element.15, f32[128,1792]{1,0:T(8,128)S(1)} %fusion.21), kind=kOutput, calls=%fused_computation.47 | convolution fusion | flops 3760390144 | bytes 36306944 | tf_op jit(solution)/shard_map/dot_general | solution.py:23
  295.7 17.2 %convolution_add_fusion = f32[128,8192]{1,0:T(8,128)} fusion(f32[128,8192]{1,0:T(8,128)S(1)} %fusion.12, bf16[8192,1792]{1,0:T(8,128)(2,1)} %param.9, f32[128,1792]{1,0:T(8,128)S(1)} %get-tuple-element.7, f32[128,1792]{1,0:T(8,128)S(1)} %fusion.21), kind=kOutput, calls=%fused_computation.2 | convolution fusion | flops 3760521216 | bytes 39583744 | tf_op jit(solution)/shard_map/dot_general | solution.py:23
  312.9 19.3 %fusion.4 = f32[128,8192]{1,0:T(8,128)} fusion(f32[128,8192]{1,0:T(8,128)} %convolution_add_fusion, f32[128,8192]{1,0:T(8,128)} %convolution_add_fusion.1, f32[128,8192]{1,0:T(8,128)} %convolution_add_fusion.2, f32[128,8192]{1,0:T(8,128)} %fusion.9, bf16[8192,1792]{1,0:T(8,128)(2,1)} %param.9, f32[128,1792]{1,0:T(8,128)S(1)} %copy-done.1, ...), kind=kOutput, calls=%fused_computation.8 | convolution fusion | flops 3763666944 | bytes 52166656 | tf_op jit(solution)/shard_map/dot_general | solution.py:23
  332.8 74.9 %reduce-scatter.2.cloned.1.call-done = f32[128,512]{1,0:T(8,128)} async-done(((f32[128,8192]{1,0:T(8,128)}), f32[128,512]{1,0:T(8,128)}) %reduce-scatter.2.cloned.1.call-update) | async-done | bytes 262160 | tf_op jit(solution)/shard_map/reduce_scatter | solution.py:68
  (92 shorter events, 34.2 us)
Async XLA Ops:
  7.2 105.1 %all-gather.2.cloned.1.call-start = ((), (), s32[]{:S(2)}) async-start(), calls=%async_computation.1 | async-start | bytes 2228224 | tf_op jit(solution)/shard_map/all_gather | solution.py:32
  7.9 399.9 %reduce-scatter.2.cloned.1.call-start = ((), (), s32[]{:S(2)}) async-start(), calls=%async_computation.2 | async-start | bytes 4456448 | tf_op jit(solution)/shard_map/reduce_scatter | solution.py:68
  7.9 12.7 %collective-permute-start = (bf16[4,128,512]{2,1,0:T(8,128)(2,1)}, bf16[4,128,512]{2,1,0:T(8,128)(2,1)S(1)}, u32[]{:S(2)}, u32[]{:S(2)}) collective-permute-start(bf16[4,128,512]{2,1,0:T(8,128)(2,1)} %param.11), channel_id=1, source_target_pairs={{0,1},{1,2},{2,3},{3,4},{4,5},{5,6},{6,7},{7,8},{8,9},{9,10},{10,1... | collective-permute-start | bytes 1572872 | tf_op jit(solution)/shard_map/ppermute | solution.py:15
  8.4 16.1 %collective-permute-start.8 = (bf16[4,128,512]{2,1,0:T(8,128)(2,1)}, bf16[4,128,512]{2,1,0:T(8,128)(2,1)S(1)}, u32[]{:S(2)}, u32[]{:S(2)}) collective-permute-start(bf16[4,128,512]{2,1,0:T(8,128)(2,1)} %param.11), channel_id=1, source_target_pairs={{0,15},{1,0},{2,1},{3,2},{4,3},{5,4},{6,5},{7,6},{8,7},{9,8},{10,9... | collective-permute-start | bytes 1572872 | tf_op jit(solution)/shard_map/ppermute | solution.py:17
  20.6 15.5 %collective-permute-start.1 = (bf16[4,128,512]{2,1,0:T(8,128)(2,1)S(1)}, bf16[4,128,512]{2,1,0:T(8,128)(2,1)S(1)}, u32[]{:S(2)}, u32[]{:S(2)}) collective-permute-start(bf16[4,128,512]{2,1,0:T(8,128)(2,1)S(1)} %collective-permute-done), channel_id=1, source_target_pairs={{0,1},{1,2},{2,3},{3,4},{4,5},{5,6},{6,7},{7,8},{8,9},{9,10},{10,1... | collective-permute-start | bytes 1572872 | tf_op jit(solution)/shard_map/ppermute | solution.py:15
  24.5 13.5 %collective-permute-start.9 = (bf16[4,128,512]{2,1,0:T(8,128)(2,1)S(1)}, bf16[4,128,512]{2,1,0:T(8,128)(2,1)S(1)}, u32[]{:S(2)}, u32[]{:S(2)}) collective-permute-start(bf16[4,128,512]{2,1,0:T(8,128)(2,1)S(1)} %collective-permute-done.8), channel_id=1, source_target_pairs={{0,15},{1,0},{2,1},{3,2},{4,3},{5,4},{6,5},{7,6},{8,7},{9,8},{10,9... | collective-permute-start | bytes 1572872 | tf_op jit(solution)/shard_map/ppermute | solution.py:17
  36.1 20.9 %copy-start.4 = (bf16[4,128,512]{2,1,0:T(8,128)(2,1)}, bf16[4,128,512]{2,1,0:T(8,128)(2,1)S(1)}, u32[]{:S(2)}) copy-start(bf16[4,128,512]{2,1,0:T(8,128)(2,1)S(1)} %collective-permute-done.1) | copy-start | bytes 1572868
  36.1 11.4 %collective-permute-start.2 = (bf16[4,128,512]{2,1,0:T(8,128)(2,1)S(1)}, bf16[4,128,512]{2,1,0:T(8,128)(2,1)S(1)}, u32[]{:S(2)}, u32[]{:S(2)}) collective-permute-start(bf16[4,128,512]{2,1,0:T(8,128)(2,1)S(1)} %collective-permute-done.1), channel_id=1, source_target_pairs={{0,1},{1,2},{2,3},{3,4},{4,5},{5,6},{6,7},{7,8},{8,9},{9,10},{10,1... | collective-permute-start | bytes 1572872 | tf_op jit(solution)/shard_map/ppermute | solution.py:15
  38.0 19.1 %collective-permute-start.10 = (bf16[4,128,512]{2,1,0:T(8,128)(2,1)S(1)}, bf16[4,128,512]{2,1,0:T(8,128)(2,1)S(1)}, u32[]{:S(2)}, u32[]{:S(2)}) collective-permute-start(bf16[4,128,512]{2,1,0:T(8,128)(2,1)S(1)} %collective-permute-done.9), channel_id=1, source_target_pairs={{0,15},{1,0},{2,1},{3,2},{4,3},{5,4},{6,5},{7,6},{8,7},{9,8},{10,9... | collective-permute-start | bytes 1572872 | tf_op jit(solution)/shard_map/ppermute | solution.py:17
  47.6 23.2 %copy-start.8 = (bf16[4,128,512]{2,1,0:T(8,128)(2,1)}, bf16[4,128,512]{2,1,0:T(8,128)(2,1)S(1)}, u32[]{:S(2)}) copy-start(bf16[4,128,512]{2,1,0:T(8,128)(2,1)S(1)} %collective-permute-done.2) | copy-start | bytes 1572868
  47.6 14.3 %collective-permute-start.3 = (bf16[4,128,512]{2,1,0:T(8,128)(2,1)S(1)}, bf16[4,128,512]{2,1,0:T(8,128)(2,1)S(1)}, u32[]{:S(2)}, u32[]{:S(2)}) collective-permute-start(bf16[4,128,512]{2,1,0:T(8,128)(2,1)S(1)} %collective-permute-done.2), channel_id=1, source_target_pairs={{0,1},{1,2},{2,3},{3,4},{4,5},{5,6},{6,7},{7,8},{8,9},{9,10},{10,1... | collective-permute-start | bytes 1572872 | tf_op jit(solution)/shard_map/ppermute | solution.py:15
  57.1 13.7 %collective-permute-start.11 = (bf16[4,128,512]{2,1,0:T(8,128)(2,1)S(1)}, bf16[4,128,512]{2,1,0:T(8,128)(2,1)S(1)}, u32[]{:S(2)}, u32[]{:S(2)}) collective-permute-start(bf16[4,128,512]{2,1,0:T(8,128)(2,1)S(1)} %collective-permute-done.10), channel_id=1, source_target_pairs={{0,15},{1,0},{2,1},{3,2},{4,3},{5,4},{6,5},{7,6},{8,7},{9,8},{10,9... | collective-permute-start | bytes 1572872 | tf_op jit(solution)/shard_map/ppermute | solution.py:17
  61.9 50.4 %copy-start.14 = (bf16[4,128,512]{2,1,0:T(8,128)(2,1)}, bf16[4,128,512]{2,1,0:T(8,128)(2,1)S(1)}, u32[]{:S(2)}) copy-start(bf16[4,128,512]{2,1,0:T(8,128)(2,1)S(1)} %collective-permute-done.3) | copy-start | bytes 1572868
  61.9 11.5 %collective-permute-start.4 = (bf16[4,128,512]{2,1,0:T(8,128)(2,1)S(1)}, bf16[4,128,512]{2,1,0:T(8,128)(2,1)S(1)}, u32[]{:S(2)}, u32[]{:S(2)}) collective-permute-start(bf16[4,128,512]{2,1,0:T(8,128)(2,1)S(1)} %collective-permute-done.3), channel_id=1, source_target_pairs={{0,1},{1,2},{2,3},{3,4},{4,5},{5,6},{6,7},{7,8},{8,9},{9,10},{10,1... | collective-permute-start | bytes 1572872 | tf_op jit(solution)/shard_map/ppermute | solution.py:15
  70.8 13.2 %collective-permute-start.12 = (bf16[4,128,512]{2,1,0:T(8,128)(2,1)S(1)}, bf16[4,128,512]{2,1,0:T(8,128)(2,1)S(1)}, u32[]{:S(2)}, u32[]{:S(2)}) collective-permute-start(bf16[4,128,512]{2,1,0:T(8,128)(2,1)S(1)} %collective-permute-done.11), channel_id=1, source_target_pairs={{0,15},{1,0},{2,1},{3,2},{4,3},{5,4},{6,5},{7,6},{8,7},{9,8},{10,9... | collective-permute-start | bytes 1572872 | tf_op jit(solution)/shard_map/ppermute | solution.py:17
  73.4 12.2 %collective-permute-start.5 = (bf16[4,128,512]{2,1,0:T(8,128)(2,1)S(1)}, bf16[4,128,512]{2,1,0:T(8,128)(2,1)S(1)}, u32[]{:S(2)}, u32[]{:S(2)}) collective-permute-start(bf16[4,128,512]{2,1,0:T(8,128)(2,1)S(1)} %collective-permute-done.4), channel_id=1, source_target_pairs={{0,1},{1,2},{2,3},{3,4},{4,5},{5,6},{6,7},{7,8},{8,9},{9,10},{10,1... | collective-permute-start | bytes 1572872 | tf_op jit(solution)/shard_map/ppermute | solution.py:15
  84.0 28.2 %copy-start.12 = (bf16[4,128,512]{2,1,0:T(8,128)(2,1)}, bf16[4,128,512]{2,1,0:T(8,128)(2,1)S(1)}, u32[]{:S(2)}) copy-start(bf16[4,128,512]{2,1,0:T(8,128)(2,1)S(1)} %collective-permute-done.12) | copy-start | bytes 1572868
  84.0 14.9 %collective-permute-start.13 = (bf16[4,128,512]{2,1,0:T(8,128)(2,1)S(1)}, bf16[4,128,512]{2,1,0:T(8,128)(2,1)}, u32[]{:S(2)}, u32[]{:S(2)}) collective-permute-start(bf16[4,128,512]{2,1,0:T(8,128)(2,1)S(1)} %collective-permute-done.12), channel_id=1, source_target_pairs={{0,15},{1,0},{2,1},{3,2},{4,3},{5,4},{6,5},{7,6},{8,7},{9,8},{10,9... | collective-permute-start | bytes 1572872 | tf_op jit(solution)/shard_map/ppermute | solution.py:17
  85.6 39.2 %copy-start.18 = (bf16[4,128,512]{2,1,0:T(8,128)(2,1)}, bf16[4,128,512]{2,1,0:T(8,128)(2,1)S(1)}, u32[]{:S(2)}) copy-start(bf16[4,128,512]{2,1,0:T(8,128)(2,1)S(1)} %collective-permute-done.5) | copy-start | bytes 1572868
  85.6 14.3 %collective-permute-start.6 = (bf16[4,128,512]{2,1,0:T(8,128)(2,1)S(1)}, bf16[4,128,512]{2,1,0:T(8,128)(2,1)}, u32[]{:S(2)}, u32[]{:S(2)}) collective-permute-start(bf16[4,128,512]{2,1,0:T(8,128)(2,1)S(1)} %collective-permute-done.5), channel_id=1, source_target_pairs={{0,1},{1,2},{2,3},{3,4},{4,5},{5,6},{6,7},{7,8},{8,9},{9,10},{10,1... | collective-permute-start | bytes 1572872 | tf_op jit(solution)/shard_map/ppermute | solution.py:15
  98.9 57.6 %collective-permute-start.14 = (bf16[4,128,512]{2,1,0:T(8,128)(2,1)}, bf16[4,128,512]{2,1,0:T(8,128)(2,1)}, u32[]{:S(2)}, u32[]{:S(2)}) collective-permute-start(bf16[4,128,512]{2,1,0:T(8,128)(2,1)} %collective-permute-done.13), channel_id=1, source_target_pairs={{0,15},{1,0},{2,1},{3,2},{4,3},{5,4},{6,5},{7,6},{8,7},{9,8},{10,9... | collective-permute-start | bytes 1572872 | tf_op jit(solution)/shard_map/ppermute | solution.py:17
  99.9 40.8 %collective-permute-start.7 = (bf16[4,128,512]{2,1,0:T(8,128)(2,1)}, bf16[4,128,512]{2,1,0:T(8,128)(2,1)}, u32[]{:S(2)}, u32[]{:S(2)}) collective-permute-start(bf16[4,128,512]{2,1,0:T(8,128)(2,1)} %collective-permute-done.6), channel_id=1, source_target_pairs={{0,1},{1,2},{2,3},{3,4},{4,5},{5,6},{6,7},{7,8},{8,9},{9,10},{10,1... | collective-permute-start | bytes 1572872 | tf_op jit(solution)/shard_map/ppermute | solution.py:15
  124.8 19.6 %copy-start.19 = (bf16[4,128,512]{2,1,0:T(8,128)(2,1)S(1)}, bf16[4,128,512]{2,1,0:T(8,128)(2,1)}, u32[]{:S(2)}) copy-start(bf16[4,128,512]{2,1,0:T(8,128)(2,1)} %copy-done.18) | copy-start | bytes 1572868
  124.8 20.5 %copy-start.17 = (bf16[4,128,512]{2,1,0:T(8,128)(2,1)S(1)}, bf16[4,128,512]{2,1,0:T(8,128)(2,1)}, u32[]{:S(2)}) copy-start(bf16[4,128,512]{2,1,0:T(8,128)(2,1)} %copy-done.16) | copy-start | bytes 1572868
  124.8 21.3 %copy-start.15 = (bf16[4,128,512]{2,1,0:T(8,128)(2,1)S(1)}, bf16[4,128,512]{2,1,0:T(8,128)(2,1)}, u32[]{:S(2)}) copy-start(bf16[4,128,512]{2,1,0:T(8,128)(2,1)} %copy-done.14) | copy-start | bytes 1572868
  124.8 22.2 %copy-start.9 = (bf16[4,128,512]{2,1,0:T(8,128)(2,1)S(1)}, bf16[4,128,512]{2,1,0:T(8,128)(2,1)}, u32[]{:S(2)}) copy-start(bf16[4,128,512]{2,1,0:T(8,128)(2,1)} %copy-done.8) | copy-start | bytes 1572868
  124.8 23.0 %copy-start.5 = (bf16[4,128,512]{2,1,0:T(8,128)(2,1)S(1)}, bf16[4,128,512]{2,1,0:T(8,128)(2,1)}, u32[]{:S(2)}) copy-start(bf16[4,128,512]{2,1,0:T(8,128)(2,1)} %copy-done.4) | copy-start | bytes 1572868
  124.9 24.7 %copy-start.3 = (bf16[4,128,512]{2,1,0:T(8,128)(2,1)S(1)}, bf16[4,128,512]{2,1,0:T(8,128)(2,1)}, u32[]{:S(2)}) copy-start(bf16[4,128,512]{2,1,0:T(8,128)(2,1)} %param.11) | copy-start | bytes 1572868
  124.9 27.2 %copy-start.7 = (bf16[4,128,512]{2,1,0:T(8,128)(2,1)S(1)}, bf16[4,128,512]{2,1,0:T(8,128)(2,1)}, u32[]{:S(2)}) copy-start(bf16[4,128,512]{2,1,0:T(8,128)(2,1)} %copy-done.6) | copy-start | bytes 1572868
  124.9 28.1 %copy-start.11 = (bf16[4,128,512]{2,1,0:T(8,128)(2,1)S(1)}, bf16[4,128,512]{2,1,0:T(8,128)(2,1)}, u32[]{:S(2)}) copy-start(bf16[4,128,512]{2,1,0:T(8,128)(2,1)} %copy-done.10) | copy-start | bytes 1572868
  124.9 28.9 %copy-start.13 = (bf16[4,128,512]{2,1,0:T(8,128)(2,1)S(1)}, bf16[4,128,512]{2,1,0:T(8,128)(2,1)}, u32[]{:S(2)}) copy-start(bf16[4,128,512]{2,1,0:T(8,128)(2,1)} %copy-done.12) | copy-start | bytes 1572868
  295.7 17.3 %copy-start.1 = (f32[128,1792]{1,0:T(8,128)S(1)}, f32[128,1792]{1,0:T(8,128)}, u32[]{:S(2)}) copy-start(f32[128,1792]{1,0:T(8,128)} %get-tuple-element.10) | copy-start | bytes 2752516
  (6 other events, 38.2 us)
Sparse Core Ops, SparseCore 0:
  10.2 56.2 all-gather.1
  332.3 75.3 reduce-scatter.1
